TPU v7x, 32 devices: a whole 2x2x4 slice. The times are simulated.
32 devices in a mesh: grp: 2 (over x), dev: 16 (over z, y, core).
Axes of the slice: x: 2, y: 2, z: 4, core: 2. Of those that a mesh axis runs over, the one named last changes fastest.
Arguments:
- coords: float32 [16384, 64], P(('grp', 'dev')), may hold values from -6 to 6
- right_side: float32 [16384, 256], P(('grp', 'dev')), may hold values from -6 to 6
- leaf_perm: int32 [32, 512], P(('grp', 'dev')), may hold values from 0 to 511, each once within a row
- near_list: int32 [32, 4], P(('grp', 'dev')), may hold values from -1 to 31, as said below
- far_leaves: int32 [32, 4], P(('grp', 'dev')), may hold values from 0 to 31, as said below
- couplings: bfloat16 [32, 4, 128, 128], P(('grp', 'dev')), may hold values from -0.5 to 0.5
- transfer: bfloat16 [32, 128, 128], P(('grp', 'dev')), may hold values from -0.5 to 0.5
- leaf_basis: bfloat16 [16384, 128], P(('grp', 'dev')), may hold values from -0.25 to 0.25
- cluster_of: int32 [32], P(('grp', 'dev')), may hold values from 0 to 7, as said below
- far_clusters: int32 [8, 4], P('grp'), may hold values from 0 to 7, as said below
- cluster_couplings: bfloat16 [8, 4, 128, 128], P('grp'), may hold values from -0.25 to 0.25
- ridge_weight: float32 [], replicated, may hold values from 0.5 to 2
Outputs:
- solution: float32 [16384, 256], P(('grp', 'dev'))
- residual: float32 [16384, 256], P(('grp', 'dev'))
Inputs may be any that keep to these rules, and one draw needn't show every extreme that they name: `near_list`: each row lists leaves of the row's group whose position within the group differs from the row's leaf by 1 to 2, each at most once, in any slot order; -1 marks an empty slot. The number of listed leaves varies from leaf to leaf. `far_leaves`: each row names 4 different leaves of the row's group whose position within the group differs from the row's leaf by more than 2 and at most 8. `cluster_of`: leaves of group g belong to clusters g * 4 to g * 4 + 3, and every cluster holds exactly 4 leaves. `far_clusters`: each row names 4 different clusters, none of them in the row's own group.
All inputs are finite; a program needn't handle non-finite values.
Results may differ from a plain program's by a relative error of at most 0.0033.
Values may be sent and summed in bfloat16 or wider, within the bound.
A program may use at most 64 MiB of HBM per device.

v0:
```python
import jax
import jax.numpy as jnp
from jax import lax
from jax.sharding import PartitionSpec as P

REACH = 2
FARREACH = 8
ITERS = 2
kernel_scale = 1.0 / 32.0
spectrum_gap = 0.5
spectrum_top = 8.0


def from_behind(shard, axis, by):
    devices = lax.axis_size(axis)
    pairs = [(i, i + by) for i in range(devices) if 0 <= i + by < devices]
    return lax.ppermute(shard, axis, pairs)


def kernel_block(left_points, right_points):
    inner_products = jnp.dot(
        left_points,
        right_points.T,
        precision=lax.Precision.HIGHEST,
        preferred_element_type=jnp.float32,
    )
    distance = (
        jnp.sum(left_points * left_points, axis=1)[:, None]
        + jnp.sum(right_points * right_points, axis=1)[None, :]
        - 2.0 * inner_products
    )
    return jnp.exp(-kernel_scale * distance).astype(jnp.bfloat16)


def body(
    coords,
    right_side,
    leaf_perm,
    near_list,
    far_leaves,
    couplings,
    transfer,
    leaf_basis,
    cluster_of,
    far_clusters,
    cluster_couplings,
    ridge_weight,
):
    dev_count = lax.axis_size("dev")
    group_index = lax.axis_index("grp")
    leaf_id = group_index * dev_count + lax.axis_index("dev")
    clusters_here = far_clusters.shape[0]
    local_cluster = cluster_of[0] - group_index * clusters_here
    ordering = leaf_perm[0]
    near_offsets = [offset for offset in range(-REACH, REACH + 1) if offset != 0]
    far_offsets = [offset for offset in range(-FARREACH, FARREACH + 1) if abs(offset) > REACH]
    neighbours = [from_behind(coords, "dev", -offset) for offset in near_offsets]
    near_flags = [
        jnp.any((near_list[0] == leaf_id + offset) & (near_list[0] >= 0)).astype(jnp.float32)
        for offset in near_offsets
    ]
    far_hits = jnp.stack(
        [far_leaves[0] == leaf_id + offset for offset in far_offsets], axis=1
    ).astype(jnp.bfloat16)
    own_block = kernel_block(coords, coords)
    near_blocks = [kernel_block(coords, neighbour_points) for neighbour_points in neighbours]
    cluster_slots = (jnp.arange(clusters_here) == local_cluster).astype(jnp.float32)

    def operate(direction):
        values = direction.astype(jnp.bfloat16)
        near_sum = jnp.dot(own_block, values, preferred_element_type=jnp.float32)
        for position in range(len(near_offsets)):
            remote = from_behind(values, "dev", -near_offsets[position])
            block_here = near_blocks[position]
            near_term = near_flags[position] * jnp.dot(
                block_here, remote, preferred_element_type=jnp.float32
            )
            near_sum = near_sum + near_term
        skeleton = lax.dot_general(
            leaf_basis,
            values[ordering],
            (((0,), (0,)), ((), ())),
            preferred_element_type=jnp.float32,
        ).astype(jnp.bfloat16)
        remote_skeletons = jnp.stack(
            [from_behind(skeleton, "dev", -offset) for offset in far_offsets]
        )
        chosen = jnp.einsum(
            "kj,jbo->kbo", far_hits, remote_skeletons, preferred_element_type=jnp.float32
        ).astype(jnp.bfloat16)
        level_one = jnp.einsum(
            "kab,kbo->ao", couplings[0], chosen, preferred_element_type=jnp.float32
        )
        uplift = lax.dot_general(
            transfer[0], skeleton, (((0,), (0,)), ((), ())), preferred_element_type=jnp.float32
        )
        contrib = cluster_slots[:, None, None] * uplift[None]
        column_sums = lax.psum_scatter(contrib, "dev", scatter_dimension=2, tiled=True).astype(
            jnp.bfloat16
        )
        every_column = lax.all_gather(column_sums, "grp", axis=0, tiled=True)
        picked = every_column[far_clusters]
        partial_coupled = jnp.einsum(
            "ckab,ckbo->cao", cluster_couplings, picked, preferred_element_type=jnp.float32
        ).astype(jnp.bfloat16)
        whole_columns = lax.all_gather(partial_coupled, "dev", axis=2, tiled=True)
        coupled = whole_columns[local_cluster]
        downward = jnp.dot(transfer[0], coupled, preferred_element_type=jnp.float32)
        tree_rows = jnp.dot(
            leaf_basis,
            (level_one + downward).astype(jnp.bfloat16),
            preferred_element_type=jnp.float32,
        )
        far_part = jnp.zeros_like(tree_rows).at[ordering].set(tree_rows)
        return ridge_weight * direction + (near_sum + far_part)

    bottom_edge = ridge_weight + spectrum_gap
    top_edge = ridge_weight + spectrum_top
    centre = (top_edge + bottom_edge) / 2.0
    spread = (top_edge - bottom_edge) / 2.0
    sigma_ratio = centre / spread
    contraction = 1.0 / sigma_ratio
    direction = right_side / centre
    solution = direction
    residual = right_side
    for rounds in range(ITERS):
        residual = residual - operate(direction)
        rho_next = 1.0 / (2.0 * sigma_ratio - contraction)
        direction = rho_next * contraction * direction + 2.0 * rho_next / spread * residual
        solution = solution + direction
        contraction = rho_next
    return (solution, residual)


def solution(mesh):
    placed = (
        P(("grp", "dev"), None),
        P(("grp", "dev"), None),
        P(("grp", "dev"), None),
        P(("grp", "dev"), None),
        P(("grp", "dev"), None),
        P(("grp", "dev"), None, None, None),
        P(("grp", "dev"), None, None),
        P(("grp", "dev"), None),
        P(("grp", "dev")),
        P("grp", None),
        P("grp", None, None, None),
        P(),
    )
    return jax.shard_map(
        body,
        mesh=mesh,
        in_specs=placed,
        out_specs=(P(("grp", "dev"), None), P(("grp", "dev"), None)),
        check_vma=False,
    )
```

profile of v0, /device:TPU:0, one launch (start us, length us, event | category | flops | bytes accessed | tf_op | source)
XLA Modules:
  0.0 243.9 jit_solution(6696561927409434020)
XLA Ops:
  12.0 6.0 %collective-permute-start.8 = (bf16[128,256]{0,1:T(8,128)(2,1)S(1)}, bf16[128,256]{0,1:T(8,128)(2,1)S(1)}, u32[]{:S(2)}, u32[]{:S(2)}) collective-permute-start(bf16[128,256]{0,1:T(8,128)(2,1)S(1)} %bitcast.186), channel_id=1, source_target_pairs={{0,8},{1,9},{2,10},{3,11},{4,12},{5,13},{6,14},{7,15},{16,24},{17,... | collective-permute-start | bytes 196616 | tf_op jit(solution)/shard_map/ppermute | solution.py:17
  18.0 3.6 %collective-permute-start.9 = (bf16[128,256]{0,1:T(8,128)(2,1)S(1)}, bf16[128,256]{0,1:T(8,128)(2,1)S(1)}, u32[]{:S(2)}, u32[]{:S(2)}) collective-permute-start(bf16[128,256]{0,1:T(8,128)(2,1)S(1)} %bitcast.187), channel_id=1, source_target_pairs={{0,7},{1,8},{2,9},{3,10},{4,11},{5,12},{6,13},{7,14},{8,15},{16,23... | collective-permute-start | bytes 196616 | tf_op jit(solution)/shard_map/ppermute | solution.py:17
  21.6 2.1 collective-permute-start.10
  34.3 2.2 fusion.3
  38.8 2.9 %collective-permute-start.13 = (bf16[128,256]{0,1:T(8,128)(2,1)S(1)}, bf16[128,256]{0,1:T(8,128)(2,1)S(1)}, u32[]{:S(2)}, u32[]{:S(2)}) collective-permute-start(bf16[128,256]{0,1:T(8,128)(2,1)S(1)} %bitcast.191), channel_id=1, source_target_pairs={{0,3},{1,4},{2,5},{3,6},{4,7},{5,8},{6,9},{7,10},{8,11},{9,12},{10... | collective-permute-start | bytes 196616 | tf_op jit(solution)/shard_map/ppermute | solution.py:17
  53.9 2.8 %collective-permute-start.1 = (bf16[512,256]{1,0:T(8,128)(2,1)S(1)}, bf16[512,256]{1,0:T(8,128)(2,1)}, u32[]{:S(2)}, u32[]{:S(2)}) collective-permute-start(bf16[512,256]{1,0:T(8,128)(2,1)S(1)} %fusion.53), channel_id=1, source_target_pairs={{0,2},{1,3},{2,4},{3,5},{4,6},{5,7},{6,8},{7,9},{8,10},{9,11},{10,... | collective-permute-start | bytes 786440 | tf_op jit(solution)/shard_map/ppermute | solution.py:17
  57.4 5.4 %collective-permute-start = (f32[512,64]{0,1:T(8,128)}, f32[512,64]{0,1:T(8,128)S(1)}, u32[]{:S(2)}, u32[]{:S(2)}) collective-permute-start(f32[512,64]{0,1:T(8,128)} %param.12), channel_id=1, source_target_pairs={{0,2},{1,3},{2,4},{3,5},{4,6},{5,7},{6,8},{7,9},{8,10},{9,11},{10,... | collective-permute-start | bytes 393224 | tf_op jit(solution)/shard_map/ppermute | solution.py:17
  63.4 2.8 %collective-permute-start.3 = (bf16[512,256]{1,0:T(8,128)(2,1)S(1)}, bf16[512,256]{1,0:T(8,128)(2,1)}, u32[]{:S(2)}, u32[]{:S(2)}) collective-permute-start(bf16[512,256]{1,0:T(8,128)(2,1)S(1)} %fusion.53), channel_id=1, source_target_pairs={{0,1},{1,2},{2,3},{3,4},{4,5},{5,6},{6,7},{7,8},{8,9},{9,10},{10,1... | collective-permute-start | bytes 786440 | tf_op jit(solution)/shard_map/ppermute | solution.py:17
  66.8 4.2 %collective-permute-start.2 = (f32[512,64]{0,1:T(8,128)}, f32[512,64]{0,1:T(8,128)}, u32[]{:S(2)}, u32[]{:S(2)}) collective-permute-start(f32[512,64]{0,1:T(8,128)} %param.12), channel_id=1, source_target_pairs={{0,1},{1,2},{2,3},{3,4},{4,5},{5,6},{6,7},{7,8},{8,9},{9,10},{10,1... | collective-permute-start | bytes 393224 | tf_op jit(solution)/shard_map/ppermute | solution.py:17
  73.5 2.0 copy.32
  78.1 2.1 exponential_convert_fusion.3
  82.4 2.1 exponential_convert_fusion.2
  87.1 2.1 exponential_convert_fusion
  89.3 2.9 %exponential_convert_fusion.1 = bf16[512,512]{1,0:T(8,128)(2,1)} fusion(f32[512]{0:T(512)S(1)} %multiply_reduce_fusion.1, f32[512,64]{0,1:T(8,128)} %param.12, f32[512,64]{0,1:T(8,128)S(1)} %collective-permute-done.4, f32[512]{0:T(512)S(1)} %copy-done.15), kind=kOutput, calls=%fused_computation.58 | convolution fusion | flops 202637312 | bytes 790528 | tf_op jit(solution)/shard_map/dot_general | solution.py:21
  94.7 2.0 fusion.16
  97.6 4.4 %all_gather.12 = bf16[8,128,16]{1,2,0:T(8,128)(2,1)S(1)} all-gather(bf16[4,128,16]{1,2,0:T(8,128)(2,1)S(1)} %convert_element_type.99), channel_id=1, replica_groups=mesh['grp'=2,'dev'=16] {'grp'}, dimensions={0}, use_global_device_ids=true | all-gather | bytes 49152 | tf_op jit(solution)/shard_map/all_gather | solution.py:101
  102.8 28.1 %all_gather.13 = bf16[4,128,256]{1,2,0:T(8,128)(2,1)S(1)} all-gather(bf16[4,128,16]{1,2,0:T(8,128)(2,1)S(1)} %fusion.23), channel_id=1, replica_groups=mesh['grp'=2,'dev'=16] {'dev'}, dimensions={2}, use_global_device_ids=true | all-gather | bytes 278528 | tf_op jit(solution)/shard_map/all_gather | solution.py:106
  132.2 2.9 %scatter_custom_fusion = f32[512,256]{1,0:T(8,128)S(1)} fusion(s32[512]{0:T(512)S(1)} %bitcast.211, f32[512,256]{1,0:T(8,128)} %copy.34, f32[]{:T(128)} %constant.33.clone.1), kind=kCustom, calls=%fused_computation.70 | custom fusion | bytes 524800 | tf_op jit(solution)/shard_map/scatter | solution.py:114
  135.2 2.4 %fusion.24 = (bf16[512,256]{1,0:T(8,128)(2,1)S(1)}, f32[512,256]{1,0:T(8,128)}) fusion(f32[]{:T(128)S(6)} %div.37, f32[]{:T(128)S(6)} %mul.171, f32[512,256]{1,0:T(8,128)S(1)} %copy-done.10, f32[]{:T(128)S(6)} %div.30, f32[512,256]{1,0:T(8,128)S(1)} %scatter_custom_fusion, f32[512,256]{1,0:T(8,128)S(1)} %convolution_multiply_fusion.9, ...), kind=kOutput, calls=%fused_computation.63 | convolution fusion | flops 135790592 | bytes 3670036 | tf_op jit(solution)/shard_map/dot_general | solution.py:75
  137.9 2.0 collective-permute-start.20
  139.9 2.9 %collective-permute-start.21 = (bf16[512,256]{1,0:T(8,128)(2,1)S(1)}, bf16[512,256]{1,0:T(8,128)(2,1)}, u32[]{:S(2)}, u32[]{:S(2)}) collective-permute-start(bf16[512,256]{1,0:T(8,128)(2,1)S(1)} %get-tuple-element.18), channel_id=1, source_target_pairs={{0,1},{1,2},{2,3},{3,4},{4,5},{5,6},{6,7},{7,8},{8,9},{9,10},{10,1... | collective-permute-start | bytes 786440 | tf_op jit(solution)/shard_map/ppermute | solution.py:17
  147.7 2.3 collective-permute-start.26
  153.5 2.3 collective-permute-start.28
  156.5 3.0 %collective-permute-start.29 = (bf16[128,256]{0,1:T(8,128)(2,1)S(1)}, bf16[128,256]{0,1:T(8,128)(2,1)S(1)}, u32[]{:S(2)}, u32[]{:S(2)}) collective-permute-start(bf16[128,256]{0,1:T(8,128)(2,1)S(1)} %bitcast.203), channel_id=1, source_target_pairs={{0,3},{1,4},{2,5},{3,6},{4,7},{5,8},{6,9},{7,10},{8,11},{9,12},{10... | collective-permute-start | bytes 196616 | tf_op jit(solution)/shard_map/ppermute | solution.py:17
  173.5 2.0 collective-permute-done.33
  179.3 5.8 %collective-permute-done.35 = bf16[128,256]{0,1:T(8,128)(2,1)S(1)} collective-permute-done((bf16[128,256]{0,1:T(8,128)(2,1)S(1)}, bf16[128,256]{0,1:T(8,128)(2,1)S(1)}, u32[]{:S(2)}, u32[]{:S(2)}) %collective-permute-start.35) | collective-permute-done | bytes 65568 | tf_op jit(solution)/shard_map/ppermute | solution.py:17
  185.7 2.0 copy.35
  193.5 11.7 %reduce-scatter.5.cloned.1.call-done = f32[4,128,16]{1,2,0:T(8,128)} async-done(((f32[4,128,256]{1,2,0:T(8,128)}), f32[4,128,16]{1,2,0:T(8,128)}) %reduce-scatter.5.cloned.1.call-update) | async-done | bytes 32784 | tf_op jit(solution)/shard_map/reduce_scatter | solution.py:98
  206.0 4.4 %all_gather.14 = bf16[8,128,16]{1,2,0:T(8,128)(2,1)S(1)} all-gather(bf16[4,128,16]{1,2,0:T(8,128)(2,1)S(1)} %convert_element_type.107), channel_id=1, replica_groups=mesh['grp'=2,'dev'=16] {'grp'}, dimensions={0}, use_global_device_ids=true | all-gather | bytes 49152 | tf_op jit(solution)/shard_map/all_gather | solution.py:101
  211.2 20.3 %all_gather.15 = bf16[4,128,256]{1,2,0:T(8,128)(2,1)S(1)} all-gather(bf16[4,128,16]{1,2,0:T(8,128)(2,1)S(1)} %fusion.22), channel_id=1, replica_groups=mesh['grp'=2,'dev'=16] {'dev'}, dimensions={2}, use_global_device_ids=true | all-gather | bytes 278528 | tf_op jit(solution)/shard_map/all_gather | solution.py:106
  232.0 2.4 scatter_custom_fusion.1
  234.4 2.7 %add_add_fusion = (f32[512,256]{1,0:T(8,128)}, f32[512,256]{1,0:T(8,128)}) fusion(f32[512,256]{1,0:T(8,128)} %get-tuple-element.19, f32[]{:T(128)S(6)} %div.39, f32[]{:T(128)S(6)} %mul.207, f32[]{:T(128)S(6)} %div.37, f32[]{:T(128)S(6)} %mul.171, f32[512,256]{1,0:T(8,128)S(1)} %copy-done.11, f32[]{:T(128)S(6)} %div.30, ...), kind=kOutput, calls=%fused_computation.61 | convolution fusion | flops 136314880 | bytes 4456476 | tf_op jit(solution)/shard_map/dot_general | solution.py:75
  (186 shorter events, 78.2 us)
Async XLA Ops:
  7.2 89.6 %reduce-scatter.3.cloned.1.call-start = ((), (), s32[]{:S(2)}) async-start(), calls=%async_computation.2 | async-start | bytes 557056 | tf_op jit(solution)/shard_map/reduce_scatter | solution.py:98
  12.0 26.9 %collective-permute-start.8 = (bf16[128,256]{0,1:T(8,128)(2,1)S(1)}, bf16[128,256]{0,1:T(8,128)(2,1)S(1)}, u32[]{:S(2)}, u32[]{:S(2)}) collective-permute-start(bf16[128,256]{0,1:T(8,128)(2,1)S(1)} %bitcast.186), channel_id=1, source_target_pairs={{0,8},{1,9},{2,10},{3,11},{4,12},{5,13},{6,14},{7,15},{16,24},{17,... | collective-permute-start | bytes 196616 | tf_op jit(solution)/shard_map/ppermute | solution.py:17
  18.0 24.4 %collective-permute-start.9 = (bf16[128,256]{0,1:T(8,128)(2,1)S(1)}, bf16[128,256]{0,1:T(8,128)(2,1)S(1)}, u32[]{:S(2)}, u32[]{:S(2)}) collective-permute-start(bf16[128,256]{0,1:T(8,128)(2,1)S(1)} %bitcast.187), channel_id=1, source_target_pairs={{0,7},{1,8},{2,9},{3,10},{4,11},{5,12},{6,13},{7,14},{8,15},{16,23... | collective-permute-start | bytes 196616 | tf_op jit(solution)/shard_map/ppermute | solution.py:17
  21.6 22.7 %collective-permute-start.10 = (bf16[128,256]{0,1:T(8,128)(2,1)S(1)}, bf16[128,256]{0,1:T(8,128)(2,1)S(1)}, u32[]{:S(2)}, u32[]{:S(2)}) collective-permute-start(bf16[128,256]{0,1:T(8,128)(2,1)S(1)} %bitcast.188), channel_id=1, source_target_pairs={{0,6},{1,7},{2,8},{3,9},{4,10},{5,11},{6,12},{7,13},{8,14},{9,15},... | collective-permute-start | bytes 196616 | tf_op jit(solution)/shard_map/ppermute | solution.py:17
  23.7 22.5 %collective-permute-start.11 = (bf16[128,256]{0,1:T(8,128)(2,1)S(1)}, bf16[128,256]{0,1:T(8,128)(2,1)S(1)}, u32[]{:S(2)}, u32[]{:S(2)}) collective-permute-start(bf16[128,256]{0,1:T(8,128)(2,1)S(1)} %bitcast.189), channel_id=1, source_target_pairs={{0,5},{1,6},{2,7},{3,8},{4,9},{5,10},{6,11},{7,12},{8,13},{9,14},{... | collective-permute-start | bytes 196616 | tf_op jit(solution)/shard_map/ppermute | solution.py:17
  25.0 23.1 %collective-permute-start.12 = (bf16[128,256]{0,1:T(8,128)(2,1)S(1)}, bf16[128,256]{0,1:T(8,128)(2,1)S(1)}, u32[]{:S(2)}, u32[]{:S(2)}) collective-permute-start(bf16[128,256]{0,1:T(8,128)(2,1)S(1)} %bitcast.190), channel_id=1, source_target_pairs={{0,4},{1,5},{2,6},{3,7},{4,8},{5,9},{6,10},{7,11},{8,12},{9,13},{1... | collective-permute-start | bytes 196616 | tf_op jit(solution)/shard_map/ppermute | solution.py:17
  28.4 176.8 %reduce-scatter.5.cloned.1.call-start = ((), (), s32[]{:S(2)}) async-start(), calls=%async_computation.3 | async-start | bytes 557056 | tf_op jit(solution)/shard_map/reduce_scatter | solution.py:98
  38.8 11.2 %collective-permute-start.13 = (bf16[128,256]{0,1:T(8,128)(2,1)S(1)}, bf16[128,256]{0,1:T(8,128)(2,1)S(1)}, u32[]{:S(2)}, u32[]{:S(2)}) collective-permute-start(bf16[128,256]{0,1:T(8,128)(2,1)S(1)} %bitcast.191), channel_id=1, source_target_pairs={{0,3},{1,4},{2,5},{3,6},{4,7},{5,8},{6,9},{7,10},{8,11},{9,12},{10... | collective-permute-start | bytes 196616 | tf_op jit(solution)/shard_map/ppermute | solution.py:17
  42.4 9.6 %collective-permute-start.14 = (bf16[128,256]{0,1:T(8,128)(2,1)S(1)}, bf16[128,256]{0,1:T(8,128)(2,1)S(1)}, u32[]{:S(2)}, u32[]{:S(2)}) collective-permute-start(bf16[128,256]{0,1:T(8,128)(2,1)S(1)} %bitcast.192), channel_id=1, source_target_pairs={{3,0},{4,1},{5,2},{6,3},{7,4},{8,5},{9,6},{10,7},{11,8},{12,9},{13... | collective-permute-start | bytes 196616 | tf_op jit(solution)/shard_map/ppermute | solution.py:17
  44.3 9.6 %collective-permute-start.15 = (bf16[128,256]{0,1:T(8,128)(2,1)S(1)}, bf16[128,256]{0,1:T(8,128)(2,1)S(1)}, u32[]{:S(2)}, u32[]{:S(2)}) collective-permute-start(bf16[128,256]{0,1:T(8,128)(2,1)S(1)} %bitcast.193), channel_id=1, source_target_pairs={{4,0},{5,1},{6,2},{7,3},{8,4},{9,5},{10,6},{11,7},{12,8},{13,9},{1... | collective-permute-start | bytes 196616 | tf_op jit(solution)/shard_map/ppermute | solution.py:17
  46.2 11.1 %collective-permute-start.16 = (bf16[128,256]{0,1:T(8,128)(2,1)S(1)}, bf16[128,256]{0,1:T(8,128)(2,1)S(1)}, u32[]{:S(2)}, u32[]{:S(2)}) collective-permute-start(bf16[128,256]{0,1:T(8,128)(2,1)S(1)} %bitcast.194), channel_id=1, source_target_pairs={{5,0},{6,1},{7,2},{8,3},{9,4},{10,5},{11,6},{12,7},{13,8},{14,9},{... | collective-permute-start | bytes 196616 | tf_op jit(solution)/shard_map/ppermute | solution.py:17
  48.1 15.2 %collective-permute-start.17 = (bf16[128,256]{0,1:T(8,128)(2,1)S(1)}, bf16[128,256]{0,1:T(8,128)(2,1)S(1)}, u32[]{:S(2)}, u32[]{:S(2)}) collective-permute-start(bf16[128,256]{0,1:T(8,128)(2,1)S(1)} %bitcast.195), channel_id=1, source_target_pairs={{6,0},{7,1},{8,2},{9,3},{10,4},{11,5},{12,6},{13,7},{14,8},{15,9},... | collective-permute-start | bytes 196616 | tf_op jit(solution)/shard_map/ppermute | solution.py:17
  50.1 16.8 %collective-permute-start.18 = (bf16[128,256]{0,1:T(8,128)(2,1)S(1)}, bf16[128,256]{0,1:T(8,128)(2,1)S(1)}, u32[]{:S(2)}, u32[]{:S(2)}) collective-permute-start(bf16[128,256]{0,1:T(8,128)(2,1)S(1)} %bitcast.196), channel_id=1, source_target_pairs={{7,0},{8,1},{9,2},{10,3},{11,4},{12,5},{13,6},{14,7},{15,8},{23,16... | collective-permute-start | bytes 196616 | tf_op jit(solution)/shard_map/ppermute | solution.py:17
  52.0 19.6 %collective-permute-start.19 = (bf16[128,256]{0,1:T(8,128)(2,1)S(1)}, bf16[128,256]{0,1:T(8,128)(2,1)S(1)}, u32[]{:S(2)}, u32[]{:S(2)}) collective-permute-start(bf16[128,256]{0,1:T(8,128)(2,1)S(1)} %bitcast.197), channel_id=1, source_target_pairs={{8,0},{9,1},{10,2},{11,3},{12,4},{13,5},{14,6},{15,7},{24,16},{25,... | collective-permute-start | bytes 196616 | tf_op jit(solution)/shard_map/ppermute | solution.py:17
  53.9 38.3 %collective-permute-start.1 = (bf16[512,256]{1,0:T(8,128)(2,1)S(1)}, bf16[512,256]{1,0:T(8,128)(2,1)}, u32[]{:S(2)}, u32[]{:S(2)}) collective-permute-start(bf16[512,256]{1,0:T(8,128)(2,1)S(1)} %fusion.53), channel_id=1, source_target_pairs={{0,2},{1,3},{2,4},{3,5},{4,6},{5,7},{6,8},{7,9},{8,10},{9,11},{10,... | collective-permute-start | bytes 786440 | tf_op jit(solution)/shard_map/ppermute | solution.py:17
  57.4 19.4 %collective-permute-start = (f32[512,64]{0,1:T(8,128)}, f32[512,64]{0,1:T(8,128)S(1)}, u32[]{:S(2)}, u32[]{:S(2)}) collective-permute-start(f32[512,64]{0,1:T(8,128)} %param.12), channel_id=1, source_target_pairs={{0,2},{1,3},{2,4},{3,5},{4,6},{5,7},{6,8},{7,9},{8,10},{9,11},{10,... | collective-permute-start | bytes 393224 | tf_op jit(solution)/shard_map/ppermute | solution.py:17
  63.4 31.3 %collective-permute-start.3 = (bf16[512,256]{1,0:T(8,128)(2,1)S(1)}, bf16[512,256]{1,0:T(8,128)(2,1)}, u32[]{:S(2)}, u32[]{:S(2)}) collective-permute-start(bf16[512,256]{1,0:T(8,128)(2,1)S(1)} %fusion.53), channel_id=1, source_target_pairs={{0,1},{1,2},{2,3},{3,4},{4,5},{5,6},{6,7},{7,8},{8,9},{9,10},{10,1... | collective-permute-start | bytes 786440 | tf_op jit(solution)/shard_map/ppermute | solution.py:17
  66.8 13.4 %collective-permute-start.2 = (f32[512,64]{0,1:T(8,128)}, f32[512,64]{0,1:T(8,128)}, u32[]{:S(2)}, u32[]{:S(2)}) collective-permute-start(f32[512,64]{0,1:T(8,128)} %param.12), channel_id=1, source_target_pairs={{0,1},{1,2},{2,3},{3,4},{4,5},{5,6},{6,7},{7,8},{8,9},{9,10},{10,1... | collective-permute-start | bytes 393224 | tf_op jit(solution)/shard_map/ppermute | solution.py:17
  71.6 21.9 %collective-permute-start.7 = (bf16[512,256]{1,0:T(8,128)(2,1)S(1)}, bf16[512,256]{1,0:T(8,128)(2,1)}, u32[]{:S(2)}, u32[]{:S(2)}) collective-permute-start(bf16[512,256]{1,0:T(8,128)(2,1)S(1)} %fusion.53), channel_id=1, source_target_pairs={{2,0},{3,1},{4,2},{5,3},{6,4},{7,5},{8,6},{9,7},{10,8},{11,9},{12,... | collective-permute-start | bytes 786440 | tf_op jit(solution)/shard_map/ppermute | solution.py:17
  76.7 9.1 %collective-permute-start.6 = (f32[512,64]{0,1:T(8,128)}, f32[512,64]{0,1:T(8,128)S(1)}, u32[]{:S(2)}, u32[]{:S(2)}) collective-permute-start(f32[512,64]{0,1:T(8,128)} %param.12), channel_id=1, source_target_pairs={{2,0},{3,1},{4,2},{5,3},{6,4},{7,5},{8,6},{9,7},{10,8},{11,9},{12,... | collective-permute-start | bytes 393224 | tf_op jit(solution)/shard_map/ppermute | solution.py:17
  80.2 55.0 %collective-permute-start.5 = (bf16[512,256]{1,0:T(8,128)(2,1)S(1)}, bf16[512,256]{1,0:T(8,128)(2,1)}, u32[]{:S(2)}, u32[]{:S(2)}) collective-permute-start(bf16[512,256]{1,0:T(8,128)(2,1)S(1)} %fusion.53), channel_id=1, source_target_pairs={{1,0},{2,1},{3,2},{4,3},{5,4},{6,5},{7,6},{8,7},{9,8},{10,9},{11,1... | collective-permute-start | bytes 786440 | tf_op jit(solution)/shard_map/ppermute | solution.py:17
  137.9 50.9 %collective-permute-start.20 = (bf16[512,256]{1,0:T(8,128)(2,1)S(1)}, bf16[512,256]{1,0:T(8,128)(2,1)}, u32[]{:S(2)}, u32[]{:S(2)}) collective-permute-start(bf16[512,256]{1,0:T(8,128)(2,1)S(1)} %get-tuple-element.18), channel_id=1, source_target_pairs={{0,2},{1,3},{2,4},{3,5},{4,6},{5,7},{6,8},{7,9},{8,10},{9,11},{10,... | collective-permute-start | bytes 786440 | tf_op jit(solution)/shard_map/ppermute | solution.py:17
  139.9 52.3 %collective-permute-start.21 = (bf16[512,256]{1,0:T(8,128)(2,1)S(1)}, bf16[512,256]{1,0:T(8,128)(2,1)}, u32[]{:S(2)}, u32[]{:S(2)}) collective-permute-start(bf16[512,256]{1,0:T(8,128)(2,1)S(1)} %get-tuple-element.18), channel_id=1, source_target_pairs={{0,1},{1,2},{2,3},{3,4},{4,5},{5,6},{6,7},{7,8},{8,9},{9,10},{10,1... | collective-permute-start | bytes 786440 | tf_op jit(solution)/shard_map/ppermute | solution.py:17
  147.7 8.8 %collective-permute-start.26 = (bf16[128,256]{0,1:T(8,128)(2,1)S(1)}, bf16[128,256]{0,1:T(8,128)(2,1)S(1)}, u32[]{:S(2)}, u32[]{:S(2)}) collective-permute-start(bf16[128,256]{0,1:T(8,128)(2,1)S(1)} %bitcast.200), channel_id=1, source_target_pairs={{0,6},{1,7},{2,8},{3,9},{4,10},{5,11},{6,12},{7,13},{8,14},{9,15},... | collective-permute-start | bytes 196616 | tf_op jit(solution)/shard_map/ppermute | solution.py:17
  151.1 9.0 %collective-permute-start.27 = (bf16[128,256]{0,1:T(8,128)(2,1)S(1)}, bf16[128,256]{0,1:T(8,128)(2,1)S(1)}, u32[]{:S(2)}, u32[]{:S(2)}) collective-permute-start(bf16[128,256]{0,1:T(8,128)(2,1)S(1)} %bitcast.201), channel_id=1, source_target_pairs={{0,5},{1,6},{2,7},{3,8},{4,9},{5,10},{6,11},{7,12},{8,13},{9,14},{... | collective-permute-start | bytes 196616 | tf_op jit(solution)/shard_map/ppermute | solution.py:17
  153.5 8.5 %collective-permute-start.28 = (bf16[128,256]{0,1:T(8,128)(2,1)S(1)}, bf16[128,256]{0,1:T(8,128)(2,1)S(1)}, u32[]{:S(2)}, u32[]{:S(2)}) collective-permute-start(bf16[128,256]{0,1:T(8,128)(2,1)S(1)} %bitcast.202), channel_id=1, source_target_pairs={{0,4},{1,5},{2,6},{3,7},{4,8},{5,9},{6,10},{7,11},{8,12},{9,13},{1... | collective-permute-start | bytes 196616 | tf_op jit(solution)/shard_map/ppermute | solution.py:17
  164.0 7.6 %collective-permute-start.32 = (bf16[128,256]{0,1:T(8,128)(2,1)S(1)}, bf16[128,256]{0,1:T(8,128)(2,1)S(1)}, u32[]{:S(2)}, u32[]{:S(2)}) collective-permute-start(bf16[128,256]{0,1:T(8,128)(2,1)S(1)} %bitcast.206), channel_id=1, source_target_pairs={{5,0},{6,1},{7,2},{8,3},{9,4},{10,5},{11,6},{12,7},{13,8},{14,9},{... | collective-permute-start | bytes 196616 | tf_op jit(solution)/shard_map/ppermute | solution.py:17
  165.9 9.6 %collective-permute-start.33 = (bf16[128,256]{0,1:T(8,128)(2,1)S(1)}, bf16[128,256]{0,1:T(8,128)(2,1)S(1)}, u32[]{:S(2)}, u32[]{:S(2)}) collective-permute-start(bf16[128,256]{0,1:T(8,128)(2,1)S(1)} %bitcast.207), channel_id=1, source_target_pairs={{6,0},{7,1},{8,2},{9,3},{10,4},{11,5},{12,6},{13,7},{14,8},{15,9},... | collective-permute-start | bytes 196616 | tf_op jit(solution)/shard_map/ppermute | solution.py:17
  168.8 8.5 %collective-permute-start.34 = (bf16[128,256]{0,1:T(8,128)(2,1)S(1)}, bf16[128,256]{0,1:T(8,128)(2,1)S(1)}, u32[]{:S(2)}, u32[]{:S(2)}) collective-permute-start(bf16[128,256]{0,1:T(8,128)(2,1)S(1)} %bitcast.208), channel_id=1, source_target_pairs={{7,0},{8,1},{9,2},{10,3},{11,4},{12,5},{13,6},{14,7},{15,8},{23,16... | collective-permute-start | bytes 196616 | tf_op jit(solution)/shard_map/ppermute | solution.py:17
  171.5 13.5 %collective-permute-start.35 = (bf16[128,256]{0,1:T(8,128)(2,1)S(1)}, bf16[128,256]{0,1:T(8,128)(2,1)S(1)}, u32[]{:S(2)}, u32[]{:S(2)}) collective-permute-start(bf16[128,256]{0,1:T(8,128)(2,1)S(1)} %bitcast.209), channel_id=1, source_target_pairs={{8,0},{9,1},{10,2},{11,3},{12,4},{13,5},{14,6},{15,7},{24,16},{25,... | collective-permute-start | bytes 196616 | tf_op jit(solution)/shard_map/ppermute | solution.py:17
  175.5 15.5 %collective-permute-start.23 = (bf16[512,256]{1,0:T(8,128)(2,1)S(1)}, bf16[512,256]{1,0:T(8,128)(2,1)}, u32[]{:S(2)}, u32[]{:S(2)}) collective-permute-start(bf16[512,256]{1,0:T(8,128)(2,1)S(1)} %get-tuple-element.18), channel_id=1, source_target_pairs={{2,0},{3,1},{4,2},{5,3},{6,4},{7,5},{8,6},{9,7},{10,8},{11,9},{12,... | collective-permute-start | bytes 786440 | tf_op jit(solution)/shard_map/ppermute | solution.py:17
  177.4 57.0 %collective-permute-start.22 = (bf16[512,256]{1,0:T(8,128)(2,1)S(1)}, bf16[512,256]{1,0:T(8,128)(2,1)}, u32[]{:S(2)}, u32[]{:S(2)}) collective-permute-start(bf16[512,256]{1,0:T(8,128)(2,1)S(1)} %get-tuple-element.18), channel_id=1, source_target_pairs={{1,0},{2,1},{3,2},{4,3},{5,4},{6,5},{7,6},{8,7},{9,8},{10,9},{11,1... | collective-permute-start | bytes 786440 | tf_op jit(solution)/shard_map/ppermute | solution.py:17
  (28 other events, 246.3 us)
Sparse Core Ops, SparseCore 0:
  28.5 57.2 reduce-scatter.2
  151.2 53.9 reduce-scatter.4
where the time goes:
time: 246 us; the launch traced here: 244 us
  starting transfers between devices  72.8 us (30%)
  blocking collectives  57.2 us (23%)
  local copies, waits for them, and re-layouts  36.7 us (15%)
  matrix products  28.5 us (12%)
  waiting for transfers between devices  22.6 us (9%)
  between operations  19 us (8%)
  other arithmetic  7.11 us (3%)
    ppermute x36, starting transfers between devices, from_behind(): return lax.ppermute(shard, axis, pairs)  72.7 us
    all_gather x2, blocking collectives, operate(): whole_columns = lax.all_gather(partial_coupled, 'dev', axis=2, tiled=True)  48.4 us
    unnamed x66, local copies, waits for them, and re-layouts  18.5 us
    dot_general x8, matrix products, operate(): jnp.dot(block_here, remote, preferred_element_type=jnp.float32)  13.5 us
    reduce_scatter x2, waiting for transfers between devices, operate(): lax.psum_scatter(contrib, 'dev', scatter_dimension=2, tiled=True)  11.7 us
    dot_general x5, matrix products, kernel_block(): jnp.dot(left_points, right_points.T, precision=lax.Precision.HIGHEST, pre...  11.4 us
    ppermute x36, waiting for transfers between devices, from_behind(): return lax.ppermute(shard, axis, pairs)  10.9 us
    all_gather x2, blocking collectives, operate(): every_column = lax.all_gather(column_sums, 'grp', axis=0, tiled=True)  8.79 us
  transfers between devices with their start and end apart: 38, of which 6 were waited for; matrix products, arithmetic and copies ran while one was open for 24% of the time, Pallas kernels for 0%

commit v1 on v0

--- a/solution.py
+++ b/solution.py
@@ -103,7 +103,8 @@
         partial_coupled = jnp.einsum(
             "ckab,ckbo->cao", cluster_couplings, picked, preferred_element_type=jnp.float32
         ).astype(jnp.bfloat16)
-        whole_columns = lax.all_gather(partial_coupled, "dev", axis=2, tiled=True)
+        blocks = lax.all_gather(partial_coupled, "dev")
+        whole_columns = jnp.concatenate(blocks, axis=2)
         coupled = whole_columns[local_cluster]
         downward = jnp.dot(transfer[0], coupled, preferred_element_type=jnp.float32)
         tree_rows = jnp.dot(

time: 246 us -> 247 us (level)
  no operation moved by 1% of the time
where the time goes in v1:
time: 247 us; the launch traced here: 245 us
  starting transfers between devices  72.8 us (29%)
  blocking collectives  56.9 us (23%)
  local copies, waits for them, and re-layouts  38.2 us (15%)
  matrix products  28.5 us (12%)
  waiting for transfers between devices  22.6 us (9%)
  between operations  19 us (8%)
  other arithmetic  7.11 us (3%)
    ppermute x36, starting transfers between devices, from_behind(): return lax.ppermute(shard, axis, pairs)  72.7 us
    all_gather x2, blocking collectives, operate(): blocks = lax.all_gather(partial_coupled, 'dev')  48.1 us
    unnamed x66, local copies, waits for them, and re-layouts  19.9 us
    dot_general x8, matrix products, operate(): jnp.dot(block_here, remote, preferred_element_type=jnp.float32)  13.5 us
    reduce_scatter x2, waiting for transfers between devices, operate(): lax.psum_scatter(contrib, 'dev', scatter_dimension=2, tiled=True)  11.7 us
    dot_general x5, matrix products, kernel_block(): jnp.dot(left_points, right_points.T, precision=lax.Precision.HIGHEST, pre...  11.4 us
    ppermute x36, waiting for transfers between devices, from_behind(): return lax.ppermute(shard, axis, pairs)  10.9 us
    all_gather x2, blocking collectives, operate(): every_column = lax.all_gather(column_sums, 'grp', axis=0, tiled=True)  8.79 us
  transfers between devices with their start and end apart: 38, of which 6 were waited for; matrix products, arithmetic and copies ran while one was open for 24% of the time, Pallas kernels for 0%

profile of v1, /device:TPU:0, one launch (start us, length us, event | category | flops | bytes accessed | tf_op | source)
XLA Modules:
  0.0 245.2 jit_solution(18075444719402892215)
XLA Ops:
  12.0 6.0 %collective-permute-start.8 = (bf16[128,256]{0,1:T(8,128)(2,1)S(1)}, bf16[128,256]{0,1:T(8,128)(2,1)S(1)}, u32[]{:S(2)}, u32[]{:S(2)}) collective-permute-start(bf16[128,256]{0,1:T(8,128)(2,1)S(1)} %bitcast.198), channel_id=1, source_target_pairs={{0,8},{1,9},{2,10},{3,11},{4,12},{5,13},{6,14},{7,15},{16,24},{17,... | collective-permute-start | bytes 196616 | tf_op jit(solution)/shard_map/ppermute | solution.py:17
  18.0 3.6 %collective-permute-start.9 = (bf16[128,256]{0,1:T(8,128)(2,1)S(1)}, bf16[128,256]{0,1:T(8,128)(2,1)S(1)}, u32[]{:S(2)}, u32[]{:S(2)}) collective-permute-start(bf16[128,256]{0,1:T(8,128)(2,1)S(1)} %bitcast.199), channel_id=1, source_target_pairs={{0,7},{1,8},{2,9},{3,10},{4,11},{5,12},{6,13},{7,14},{8,15},{16,23... | collective-permute-start | bytes 196616 | tf_op jit(solution)/shard_map/ppermute | solution.py:17
  21.6 2.1 collective-permute-start.10
  34.3 2.2 fusion.3
  38.8 2.9 %collective-permute-start.13 = (bf16[128,256]{0,1:T(8,128)(2,1)S(1)}, bf16[128,256]{0,1:T(8,128)(2,1)S(1)}, u32[]{:S(2)}, u32[]{:S(2)}) collective-permute-start(bf16[128,256]{0,1:T(8,128)(2,1)S(1)} %bitcast.203), channel_id=1, source_target_pairs={{0,3},{1,4},{2,5},{3,6},{4,7},{5,8},{6,9},{7,10},{8,11},{9,12},{10... | collective-permute-start | bytes 196616 | tf_op jit(solution)/shard_map/ppermute | solution.py:17
  53.9 2.8 %collective-permute-start.1 = (bf16[512,256]{1,0:T(8,128)(2,1)S(1)}, bf16[512,256]{1,0:T(8,128)(2,1)}, u32[]{:S(2)}, u32[]{:S(2)}) collective-permute-start(bf16[512,256]{1,0:T(8,128)(2,1)S(1)} %fusion.53), channel_id=1, source_target_pairs={{0,2},{1,3},{2,4},{3,5},{4,6},{5,7},{6,8},{7,9},{8,10},{9,11},{10,... | collective-permute-start | bytes 786440 | tf_op jit(solution)/shard_map/ppermute | solution.py:17
  57.4 5.4 %collective-permute-start = (f32[512,64]{0,1:T(8,128)}, f32[512,64]{0,1:T(8,128)S(1)}, u32[]{:S(2)}, u32[]{:S(2)}) collective-permute-start(f32[512,64]{0,1:T(8,128)} %param.12), channel_id=1, source_target_pairs={{0,2},{1,3},{2,4},{3,5},{4,6},{5,7},{6,8},{7,9},{8,10},{9,11},{10,... | collective-permute-start | bytes 393224 | tf_op jit(solution)/shard_map/ppermute | solution.py:17
  63.4 2.8 %collective-permute-start.3 = (bf16[512,256]{1,0:T(8,128)(2,1)S(1)}, bf16[512,256]{1,0:T(8,128)(2,1)}, u32[]{:S(2)}, u32[]{:S(2)}) collective-permute-start(bf16[512,256]{1,0:T(8,128)(2,1)S(1)} %fusion.53), channel_id=1, source_target_pairs={{0,1},{1,2},{2,3},{3,4},{4,5},{5,6},{6,7},{7,8},{8,9},{9,10},{10,1... | collective-permute-start | bytes 786440 | tf_op jit(solution)/shard_map/ppermute | solution.py:17
  66.8 4.2 %collective-permute-start.2 = (f32[512,64]{0,1:T(8,128)}, f32[512,64]{0,1:T(8,128)}, u32[]{:S(2)}, u32[]{:S(2)}) collective-permute-start(f32[512,64]{0,1:T(8,128)} %param.12), channel_id=1, source_target_pairs={{0,1},{1,2},{2,3},{3,4},{4,5},{5,6},{6,7},{7,8},{8,9},{9,10},{10,1... | collective-permute-start | bytes 393224 | tf_op jit(solution)/shard_map/ppermute | solution.py:17
  73.5 2.0 copy.52
  78.1 2.1 exponential_convert_fusion.3
  82.4 2.1 exponential_convert_fusion.2
  87.1 2.1 exponential_convert_fusion
  89.3 2.9 %exponential_convert_fusion.1 = bf16[512,512]{1,0:T(8,128)(2,1)} fusion(f32[512]{0:T(512)S(1)} %multiply_reduce_fusion.1, f32[512,64]{0,1:T(8,128)} %param.12, f32[512,64]{0,1:T(8,128)S(1)} %collective-permute-done.4, f32[512]{0:T(512)S(1)} %copy-done.15), kind=kOutput, calls=%fused_computation.58 | convolution fusion | flops 202637312 | bytes 790528 | tf_op jit(solution)/shard_map/dot_general | solution.py:21
  94.7 2.0 fusion.16
  97.6 4.4 %all_gather.18 = bf16[8,128,16]{1,2,0:T(8,128)(2,1)S(1)} all-gather(bf16[4,128,16]{1,2,0:T(8,128)(2,1)S(1)} %convert_element_type.99), channel_id=1, replica_groups=mesh['grp'=2,'dev'=16] {'grp'}, dimensions={0}, use_global_device_ids=true | all-gather | bytes 49152 | tf_op jit(solution)/shard_map/all_gather | solution.py:101
  102.8 28.0 %all-gather = bf16[64,128,16]{1,2,0:T(8,128)(2,1)S(1)} all-gather(bf16[4,128,16]{1,2,0:T(8,128)(2,1)S(1)} %fusion.23), channel_id=2, replica_groups=mesh['grp'=2,'dev'=16] {'dev'}, dimensions={0}, use_global_device_ids=true | all-gather | bytes 278528 | tf_op jit(solution)/shard_map/all_gather | solution.py:106
  132.9 2.9 %scatter_custom_fusion = f32[512,256]{1,0:T(8,128)S(1)} fusion(s32[512]{0:T(512)S(1)} %bitcast.223, f32[512,256]{1,0:T(8,128)} %copy.55, f32[]{:T(128)} %constant.33.clone.1), kind=kCustom, calls=%fused_computation.70 | custom fusion | bytes 524800 | tf_op jit(solution)/shard_map/scatter | solution.py:115
  135.8 2.4 fusion.24
  138.5 2.0 collective-permute-start.20
  140.6 2.9 %collective-permute-start.21 = (bf16[512,256]{1,0:T(8,128)(2,1)S(1)}, bf16[512,256]{1,0:T(8,128)(2,1)}, u32[]{:S(2)}, u32[]{:S(2)}) collective-permute-start(bf16[512,256]{1,0:T(8,128)(2,1)S(1)} %get-tuple-element.18), channel_id=1, source_target_pairs={{0,1},{1,2},{2,3},{3,4},{4,5},{5,6},{6,7},{7,8},{8,9},{9,10},{10,1... | collective-permute-start | bytes 786440 | tf_op jit(solution)/shard_map/ppermute | solution.py:17
  148.4 2.2 collective-permute-start.26
  154.1 2.3 collective-permute-start.28
  157.1 3.0 %collective-permute-start.29 = (bf16[128,256]{0,1:T(8,128)(2,1)S(1)}, bf16[128,256]{0,1:T(8,128)(2,1)S(1)}, u32[]{:S(2)}, u32[]{:S(2)}) collective-permute-start(bf16[128,256]{0,1:T(8,128)(2,1)S(1)} %bitcast.215), channel_id=1, source_target_pairs={{0,3},{1,4},{2,5},{3,6},{4,7},{5,8},{6,9},{7,10},{8,11},{9,12},{10... | collective-permute-start | bytes 196616 | tf_op jit(solution)/shard_map/ppermute | solution.py:17
  174.1 2.0 collective-permute-done.33
  179.9 5.8 %collective-permute-done.35 = bf16[128,256]{0,1:T(8,128)(2,1)S(1)} collective-permute-done((bf16[128,256]{0,1:T(8,128)(2,1)S(1)}, bf16[128,256]{0,1:T(8,128)(2,1)S(1)}, u32[]{:S(2)}, u32[]{:S(2)}) %collective-permute-start.35) | collective-permute-done | bytes 65568 | tf_op jit(solution)/shard_map/ppermute | solution.py:17
  186.3 2.0 copy.56
  194.1 11.7 %reduce-scatter.5.cloned.1.call-done = f32[4,128,16]{1,2,0:T(8,128)} async-done(((f32[4,128,256]{1,2,0:T(8,128)}), f32[4,128,16]{1,2,0:T(8,128)}) %reduce-scatter.5.cloned.1.call-update) | async-done | bytes 32784 | tf_op jit(solution)/shard_map/reduce_scatter | solution.py:98
  206.6 4.4 %all_gather.21 = bf16[8,128,16]{1,2,0:T(8,128)(2,1)S(1)} all-gather(bf16[4,128,16]{1,2,0:T(8,128)(2,1)S(1)} %convert_element_type.107), channel_id=1, replica_groups=mesh['grp'=2,'dev'=16] {'grp'}, dimensions={0}, use_global_device_ids=true | all-gather | bytes 49152 | tf_op jit(solution)/shard_map/all_gather | solution.py:101
  211.8 20.1 %all-gather.1 = bf16[64,128,16]{1,2,0:T(8,128)(2,1)S(1)} all-gather(bf16[4,128,16]{1,2,0:T(8,128)(2,1)S(1)} %fusion.22), channel_id=3, replica_groups=mesh['grp'=2,'dev'=16] {'dev'}, dimensions={0}, use_global_device_ids=true | all-gather | bytes 278528 | tf_op jit(solution)/shard_map/all_gather | solution.py:106
  233.2 2.4 scatter_custom_fusion.1
  235.6 2.7 %add_add_fusion = (f32[512,256]{1,0:T(8,128)}, f32[512,256]{1,0:T(8,128)}) fusion(f32[512,256]{1,0:T(8,128)} %get-tuple-element.19, f32[]{:T(128)S(6)} %div.39, f32[]{:T(128)S(6)} %mul.207, f32[]{:T(128)S(6)} %div.37, f32[]{:T(128)S(6)} %mul.171, f32[512,256]{1,0:T(8,128)S(1)} %copy-done.11, f32[]{:T(128)S(6)} %div.30, ...), kind=kOutput, calls=%fused_computation.61 | convolution fusion | flops 136314880 | bytes 4456476 | tf_op jit(solution)/shard_map/dot_general | solution.py:75
  (188 shorter events, 79.7 us)
Async XLA Ops:
  7.2 89.6 %reduce-scatter.3.cloned.1.call-start = ((), (), s32[]{:S(2)}) async-start(), calls=%async_computation.2 | async-start | bytes 557056 | tf_op jit(solution)/shard_map/reduce_scatter | solution.py:98
  12.0 26.9 %collective-permute-start.8 = (bf16[128,256]{0,1:T(8,128)(2,1)S(1)}, bf16[128,256]{0,1:T(8,128)(2,1)S(1)}, u32[]{:S(2)}, u32[]{:S(2)}) collective-permute-start(bf16[128,256]{0,1:T(8,128)(2,1)S(1)} %bitcast.198), channel_id=1, source_target_pairs={{0,8},{1,9},{2,10},{3,11},{4,12},{5,13},{6,14},{7,15},{16,24},{17,... | collective-permute-start | bytes 196616 | tf_op jit(solution)/shard_map/ppermute | solution.py:17
  18.0 24.4 %collective-permute-start.9 = (bf16[128,256]{0,1:T(8,128)(2,1)S(1)}, bf16[128,256]{0,1:T(8,128)(2,1)S(1)}, u32[]{:S(2)}, u32[]{:S(2)}) collective-permute-start(bf16[128,256]{0,1:T(8,128)(2,1)S(1)} %bitcast.199), channel_id=1, source_target_pairs={{0,7},{1,8},{2,9},{3,10},{4,11},{5,12},{6,13},{7,14},{8,15},{16,23... | collective-permute-start | bytes 196616 | tf_op jit(solution)/shard_map/ppermute | solution.py:17
  21.6 22.7 %collective-permute-start.10 = (bf16[128,256]{0,1:T(8,128)(2,1)S(1)}, bf16[128,256]{0,1:T(8,128)(2,1)S(1)}, u32[]{:S(2)}, u32[]{:S(2)}) collective-permute-start(bf16[128,256]{0,1:T(8,128)(2,1)S(1)} %bitcast.200), channel_id=1, source_target_pairs={{0,6},{1,7},{2,8},{3,9},{4,10},{5,11},{6,12},{7,13},{8,14},{9,15},... | collective-permute-start | bytes 196616 | tf_op jit(solution)/shard_map/ppermute | solution.py:17
  23.7 22.5 %collective-permute-start.11 = (bf16[128,256]{0,1:T(8,128)(2,1)S(1)}, bf16[128,256]{0,1:T(8,128)(2,1)S(1)}, u32[]{:S(2)}, u32[]{:S(2)}) collective-permute-start(bf16[128,256]{0,1:T(8,128)(2,1)S(1)} %bitcast.201), channel_id=1, source_target_pairs={{0,5},{1,6},{2,7},{3,8},{4,9},{5,10},{6,11},{7,12},{8,13},{9,14},{... | collective-permute-start | bytes 196616 | tf_op jit(solution)/shard_map/ppermute | solution.py:17
  25.0 23.1 %collective-permute-start.12 = (bf16[128,256]{0,1:T(8,128)(2,1)S(1)}, bf16[128,256]{0,1:T(8,128)(2,1)S(1)}, u32[]{:S(2)}, u32[]{:S(2)}) collective-permute-start(bf16[128,256]{0,1:T(8,128)(2,1)S(1)} %bitcast.202), channel_id=1, source_target_pairs={{0,4},{1,5},{2,6},{3,7},{4,8},{5,9},{6,10},{7,11},{8,12},{9,13},{1... | collective-permute-start | bytes 196616 | tf_op jit(solution)/shard_map/ppermute | solution.py:17
  28.4 177.4 %reduce-scatter.5.cloned.1.call-start = ((), (), s32[]{:S(2)}) async-start(), calls=%async_computation.3 | async-start | bytes 557056 | tf_op jit(solution)/shard_map/reduce_scatter | solution.py:98
  38.8 11.2 %collective-permute-start.13 = (bf16[128,256]{0,1:T(8,128)(2,1)S(1)}, bf16[128,256]{0,1:T(8,128)(2,1)S(1)}, u32[]{:S(2)}, u32[]{:S(2)}) collective-permute-start(bf16[128,256]{0,1:T(8,128)(2,1)S(1)} %bitcast.203), channel_id=1, source_target_pairs={{0,3},{1,4},{2,5},{3,6},{4,7},{5,8},{6,9},{7,10},{8,11},{9,12},{10... | collective-permute-start | bytes 196616 | tf_op jit(solution)/shard_map/ppermute | solution.py:17
  42.4 9.6 %collective-permute-start.14 = (bf16[128,256]{0,1:T(8,128)(2,1)S(1)}, bf16[128,256]{0,1:T(8,128)(2,1)S(1)}, u32[]{:S(2)}, u32[]{:S(2)}) collective-permute-start(bf16[128,256]{0,1:T(8,128)(2,1)S(1)} %bitcast.204), channel_id=1, source_target_pairs={{3,0},{4,1},{5,2},{6,3},{7,4},{8,5},{9,6},{10,7},{11,8},{12,9},{13... | collective-permute-start | bytes 196616 | tf_op jit(solution)/shard_map/ppermute | solution.py:17
  44.3 9.6 %collective-permute-start.15 = (bf16[128,256]{0,1:T(8,128)(2,1)S(1)}, bf16[128,256]{0,1:T(8,128)(2,1)S(1)}, u32[]{:S(2)}, u32[]{:S(2)}) collective-permute-start(bf16[128,256]{0,1:T(8,128)(2,1)S(1)} %bitcast.205), channel_id=1, source_target_pairs={{4,0},{5,1},{6,2},{7,3},{8,4},{9,5},{10,6},{11,7},{12,8},{13,9},{1... | collective-permute-start | bytes 196616 | tf_op jit(solution)/shard_map/ppermute | solution.py:17
  46.2 11.1 %collective-permute-start.16 = (bf16[128,256]{0,1:T(8,128)(2,1)S(1)}, bf16[128,256]{0,1:T(8,128)(2,1)S(1)}, u32[]{:S(2)}, u32[]{:S(2)}) collective-permute-start(bf16[128,256]{0,1:T(8,128)(2,1)S(1)} %bitcast.206), channel_id=1, source_target_pairs={{5,0},{6,1},{7,2},{8,3},{9,4},{10,5},{11,6},{12,7},{13,8},{14,9},{... | collective-permute-start | bytes 196616 | tf_op jit(solution)/shard_map/ppermute | solution.py:17
  48.1 15.2 %collective-permute-start.17 = (bf16[128,256]{0,1:T(8,128)(2,1)S(1)}, bf16[128,256]{0,1:T(8,128)(2,1)S(1)}, u32[]{:S(2)}, u32[]{:S(2)}) collective-permute-start(bf16[128,256]{0,1:T(8,128)(2,1)S(1)} %bitcast.207), channel_id=1, source_target_pairs={{6,0},{7,1},{8,2},{9,3},{10,4},{11,5},{12,6},{13,7},{14,8},{15,9},... | collective-permute-start | bytes 196616 | tf_op jit(solution)/shard_map/ppermute | solution.py:17
  50.1 16.8 %collective-permute-start.18 = (bf16[128,256]{0,1:T(8,128)(2,1)S(1)}, bf16[128,256]{0,1:T(8,128)(2,1)S(1)}, u32[]{:S(2)}, u32[]{:S(2)}) collective-permute-start(bf16[128,256]{0,1:T(8,128)(2,1)S(1)} %bitcast.208), channel_id=1, source_target_pairs={{7,0},{8,1},{9,2},{10,3},{11,4},{12,5},{13,6},{14,7},{15,8},{23,16... | collective-permute-start | bytes 196616 | tf_op jit(solution)/shard_map/ppermute | solution.py:17
  52.0 19.6 %collective-permute-start.19 = (bf16[128,256]{0,1:T(8,128)(2,1)S(1)}, bf16[128,256]{0,1:T(8,128)(2,1)S(1)}, u32[]{:S(2)}, u32[]{:S(2)}) collective-permute-start(bf16[128,256]{0,1:T(8,128)(2,1)S(1)} %bitcast.209), channel_id=1, source_target_pairs={{8,0},{9,1},{10,2},{11,3},{12,4},{13,5},{14,6},{15,7},{24,16},{25,... | collective-permute-start | bytes 196616 | tf_op jit(solution)/shard_map/ppermute | solution.py:17
  53.9 38.3 %collective-permute-start.1 = (bf16[512,256]{1,0:T(8,128)(2,1)S(1)}, bf16[512,256]{1,0:T(8,128)(2,1)}, u32[]{:S(2)}, u32[]{:S(2)}) collective-permute-start(bf16[512,256]{1,0:T(8,128)(2,1)S(1)} %fusion.53), channel_id=1, source_target_pairs={{0,2},{1,3},{2,4},{3,5},{4,6},{5,7},{6,8},{7,9},{8,10},{9,11},{10,... | collective-permute-start | bytes 786440 | tf_op jit(solution)/shard_map/ppermute | solution.py:17
  57.4 19.4 %collective-permute-start = (f32[512,64]{0,1:T(8,128)}, f32[512,64]{0,1:T(8,128)S(1)}, u32[]{:S(2)}, u32[]{:S(2)}) collective-permute-start(f32[512,64]{0,1:T(8,128)} %param.12), channel_id=1, source_target_pairs={{0,2},{1,3},{2,4},{3,5},{4,6},{5,7},{6,8},{7,9},{8,10},{9,11},{10,... | collective-permute-start | bytes 393224 | tf_op jit(solution)/shard_map/ppermute | solution.py:17
  63.4 31.3 %collective-permute-start.3 = (bf16[512,256]{1,0:T(8,128)(2,1)S(1)}, bf16[512,256]{1,0:T(8,128)(2,1)}, u32[]{:S(2)}, u32[]{:S(2)}) collective-permute-start(bf16[512,256]{1,0:T(8,128)(2,1)S(1)} %fusion.53), channel_id=1, source_target_pairs={{0,1},{1,2},{2,3},{3,4},{4,5},{5,6},{6,7},{7,8},{8,9},{9,10},{10,1... | collective-permute-start | bytes 786440 | tf_op jit(solution)/shard_map/ppermute | solution.py:17
  66.8 13.4 %collective-permute-start.2 = (f32[512,64]{0,1:T(8,128)}, f32[512,64]{0,1:T(8,128)}, u32[]{:S(2)}, u32[]{:S(2)}) collective-permute-start(f32[512,64]{0,1:T(8,128)} %param.12), channel_id=1, source_target_pairs={{0,1},{1,2},{2,3},{3,4},{4,5},{5,6},{6,7},{7,8},{8,9},{9,10},{10,1... | collective-permute-start | bytes 393224 | tf_op jit(solution)/shard_map/ppermute | solution.py:17
  71.6 21.9 %collective-permute-start.7 = (bf16[512,256]{1,0:T(8,128)(2,1)S(1)}, bf16[512,256]{1,0:T(8,128)(2,1)}, u32[]{:S(2)}, u32[]{:S(2)}) collective-permute-start(bf16[512,256]{1,0:T(8,128)(2,1)S(1)} %fusion.53), channel_id=1, source_target_pairs={{2,0},{3,1},{4,2},{5,3},{6,4},{7,5},{8,6},{9,7},{10,8},{11,9},{12,... | collective-permute-start | bytes 786440 | tf_op jit(solution)/shard_map/ppermute | solution.py:17
  76.7 9.1 %collective-permute-start.6 = (f32[512,64]{0,1:T(8,128)}, f32[512,64]{0,1:T(8,128)S(1)}, u32[]{:S(2)}, u32[]{:S(2)}) collective-permute-start(f32[512,64]{0,1:T(8,128)} %param.12), channel_id=1, source_target_pairs={{2,0},{3,1},{4,2},{5,3},{6,4},{7,5},{8,6},{9,7},{10,8},{11,9},{12,... | collective-permute-start | bytes 393224 | tf_op jit(solution)/shard_map/ppermute | solution.py:17
  80.2 55.6 %collective-permute-start.5 = (bf16[512,256]{1,0:T(8,128)(2,1)S(1)}, bf16[512,256]{1,0:T(8,128)(2,1)}, u32[]{:S(2)}, u32[]{:S(2)}) collective-permute-start(bf16[512,256]{1,0:T(8,128)(2,1)S(1)} %fusion.53), channel_id=1, source_target_pairs={{1,0},{2,1},{3,2},{4,3},{5,4},{6,5},{7,6},{8,7},{9,8},{10,9},{11,1... | collective-permute-start | bytes 786440 | tf_op jit(solution)/shard_map/ppermute | solution.py:17
  138.5 50.9 %collective-permute-start.20 = (bf16[512,256]{1,0:T(8,128)(2,1)S(1)}, bf16[512,256]{1,0:T(8,128)(2,1)}, u32[]{:S(2)}, u32[]{:S(2)}) collective-permute-start(bf16[512,256]{1,0:T(8,128)(2,1)S(1)} %get-tuple-element.18), channel_id=1, source_target_pairs={{0,2},{1,3},{2,4},{3,5},{4,6},{5,7},{6,8},{7,9},{8,10},{9,11},{10,... | collective-permute-start | bytes 786440 | tf_op jit(solution)/shard_map/ppermute | solution.py:17
  140.6 52.3 %collective-permute-start.21 = (bf16[512,256]{1,0:T(8,128)(2,1)S(1)}, bf16[512,256]{1,0:T(8,128)(2,1)}, u32[]{:S(2)}, u32[]{:S(2)}) collective-permute-start(bf16[512,256]{1,0:T(8,128)(2,1)S(1)} %get-tuple-element.18), channel_id=1, source_target_pairs={{0,1},{1,2},{2,3},{3,4},{4,5},{5,6},{6,7},{7,8},{8,9},{9,10},{10,1... | collective-permute-start | bytes 786440 | tf_op jit(solution)/shard_map/ppermute | solution.py:17
  148.4 8.8 %collective-permute-start.26 = (bf16[128,256]{0,1:T(8,128)(2,1)S(1)}, bf16[128,256]{0,1:T(8,128)(2,1)S(1)}, u32[]{:S(2)}, u32[]{:S(2)}) collective-permute-start(bf16[128,256]{0,1:T(8,128)(2,1)S(1)} %bitcast.212), channel_id=1, source_target_pairs={{0,6},{1,7},{2,8},{3,9},{4,10},{5,11},{6,12},{7,13},{8,14},{9,15},... | collective-permute-start | bytes 196616 | tf_op jit(solution)/shard_map/ppermute | solution.py:17
  151.7 9.0 %collective-permute-start.27 = (bf16[128,256]{0,1:T(8,128)(2,1)S(1)}, bf16[128,256]{0,1:T(8,128)(2,1)S(1)}, u32[]{:S(2)}, u32[]{:S(2)}) collective-permute-start(bf16[128,256]{0,1:T(8,128)(2,1)S(1)} %bitcast.213), channel_id=1, source_target_pairs={{0,5},{1,6},{2,7},{3,8},{4,9},{5,10},{6,11},{7,12},{8,13},{9,14},{... | collective-permute-start | bytes 196616 | tf_op jit(solution)/shard_map/ppermute | solution.py:17
  154.1 8.5 %collective-permute-start.28 = (bf16[128,256]{0,1:T(8,128)(2,1)S(1)}, bf16[128,256]{0,1:T(8,128)(2,1)S(1)}, u32[]{:S(2)}, u32[]{:S(2)}) collective-permute-start(bf16[128,256]{0,1:T(8,128)(2,1)S(1)} %bitcast.214), channel_id=1, source_target_pairs={{0,4},{1,5},{2,6},{3,7},{4,8},{5,9},{6,10},{7,11},{8,12},{9,13},{1... | collective-permute-start | bytes 196616 | tf_op jit(solution)/shard_map/ppermute | solution.py:17
  164.6 7.6 %collective-permute-start.32 = (bf16[128,256]{0,1:T(8,128)(2,1)S(1)}, bf16[128,256]{0,1:T(8,128)(2,1)S(1)}, u32[]{:S(2)}, u32[]{:S(2)}) collective-permute-start(bf16[128,256]{0,1:T(8,128)(2,1)S(1)} %bitcast.218), channel_id=1, source_target_pairs={{5,0},{6,1},{7,2},{8,3},{9,4},{10,5},{11,6},{12,7},{13,8},{14,9},{... | collective-permute-start | bytes 196616 | tf_op jit(solution)/shard_map/ppermute | solution.py:17
  166.5 9.5 %collective-permute-start.33 = (bf16[128,256]{0,1:T(8,128)(2,1)S(1)}, bf16[128,256]{0,1:T(8,128)(2,1)S(1)}, u32[]{:S(2)}, u32[]{:S(2)}) collective-permute-start(bf16[128,256]{0,1:T(8,128)(2,1)S(1)} %bitcast.219), channel_id=1, source_target_pairs={{6,0},{7,1},{8,2},{9,3},{10,4},{11,5},{12,6},{13,7},{14,8},{15,9},... | collective-permute-start | bytes 196616 | tf_op jit(solution)/shard_map/ppermute | solution.py:17
  169.5 8.5 %collective-permute-start.34 = (bf16[128,256]{0,1:T(8,128)(2,1)S(1)}, bf16[128,256]{0,1:T(8,128)(2,1)S(1)}, u32[]{:S(2)}, u32[]{:S(2)}) collective-permute-start(bf16[128,256]{0,1:T(8,128)(2,1)S(1)} %bitcast.220), channel_id=1, source_target_pairs={{7,0},{8,1},{9,2},{10,3},{11,4},{12,5},{13,6},{14,7},{15,8},{23,16... | collective-permute-start | bytes 196616 | tf_op jit(solution)/shard_map/ppermute | solution.py:17
  172.2 13.5 %collective-permute-start.35 = (bf16[128,256]{0,1:T(8,128)(2,1)S(1)}, bf16[128,256]{0,1:T(8,128)(2,1)S(1)}, u32[]{:S(2)}, u32[]{:S(2)}) collective-permute-start(bf16[128,256]{0,1:T(8,128)(2,1)S(1)} %bitcast.221), channel_id=1, source_target_pairs={{8,0},{9,1},{10,2},{11,3},{12,4},{13,5},{14,6},{15,7},{24,16},{25,... | collective-permute-start | bytes 196616 | tf_op jit(solution)/shard_map/ppermute | solution.py:17
  176.1 15.4 %collective-permute-start.23 = (bf16[512,256]{1,0:T(8,128)(2,1)S(1)}, bf16[512,256]{1,0:T(8,128)(2,1)}, u32[]{:S(2)}, u32[]{:S(2)}) collective-permute-start(bf16[512,256]{1,0:T(8,128)(2,1)S(1)} %get-tuple-element.18), channel_id=1, source_target_pairs={{2,0},{3,1},{4,2},{5,3},{6,4},{7,5},{8,6},{9,7},{10,8},{11,9},{12,... | collective-permute-start | bytes 786440 | tf_op jit(solution)/shard_map/ppermute | solution.py:17
  178.0 57.6 %collective-permute-start.22 = (bf16[512,256]{1,0:T(8,128)(2,1)S(1)}, bf16[512,256]{1,0:T(8,128)(2,1)}, u32[]{:S(2)}, u32[]{:S(2)}) collective-permute-start(bf16[512,256]{1,0:T(8,128)(2,1)S(1)} %get-tuple-element.18), channel_id=1, source_target_pairs={{1,0},{2,1},{3,2},{4,3},{5,4},{6,5},{7,6},{8,7},{9,8},{10,9},{11,1... | collective-permute-start | bytes 786440 | tf_op jit(solution)/shard_map/ppermute | solution.py:17
  (28 other events, 199.4 us)
Sparse Core Ops, SparseCore 0:
  28.5 57.2 reduce-scatter.2
  151.8 53.9 reduce-scatter.4
